TPU v7x, 256 devices: a whole 4x4x8 slice. The times are simulated.
256 devices in a mesh: contacts: 32 (over y, z), tm: 8 (over x, core).
Axes of the slice: x: 4, y: 4, z: 8, core: 2. Of those that a mesh axis runs over, the one named last changes fastest.
Arguments:
- signal: bfloat16 [8192, 1024], P('contacts', 'tm'), may hold values from -6 to 6
- pos_idx: int32 [8192], P('contacts'), may hold values from 0 to 4095
- live_count: int32 [32], P('contacts'), may hold values from 128 to 256, as said below
- latents: bfloat16 [256, 512], replicated, may hold values from -400 to 400
- pos_table: bfloat16 [4096, 512], replicated, may hold values from -6 to 6
- w_in: bfloat16 [32, 512], replicated, may hold values from -1 to 1
- w_kv: bfloat16 [512, 1024], replicated, may hold values from -0.25 to 0.25
- w_query: bfloat16 [512, 512], replicated, may hold values from -0.25 to 0.25
- w_out: bfloat16 [512, 512], replicated, may hold values from -0.25 to 0.25
- conv_weight: bfloat16 [2, 3, 512, 512], replicated, may hold values from -0.15625 to 0.15625
- conv_bias: float32 [2, 512], replicated, may hold values from -3 to 3
- cotangent: bfloat16 [32, 256, 512], P('tm', 'contacts'), may hold values from -6 to 6
Outputs:
- features: bfloat16 [32, 256, 512], P('tm', 'contacts')
- d_latents: float32 [256, 512], replicated
Inputs may be any that keep to these rules, and one draw needn't show every extreme that they name: The first live_count[b] contacts of block b are valid; some block is full and some block has exactly 128 valid contacts.
All inputs are finite; a program needn't handle non-finite values.
Results may differ from a plain program's by a relative error of at most 0.018.
The roundings to bfloat16 on the way count: a program that leaves them out, or rounds other values in their place, can miss the bound.
Values may be sent and summed in bfloat16 or wider, within the bound.
No kernel may reach another device: no remote copies, remote signals or barrier semaphores. Data moves between devices by JAX's collectives and lax.ppermute only.
A program may use at most 192 MiB of HBM per device.

v0:
```python
import jax
import jax.numpy as jnp
from jax import lax
from jax.sharding import PartitionSpec as P

HD = 64
PATCH = 32
KSIZE = 3
LAYERS = 2
neg_big = -1e30
scale_dot = 0.125


def joined(x, axis, combine):
    everything = jax.tree.map(lambda part: lax.all_gather(part, axis), x)
    first = jax.tree.map(lambda part: part[0], everything)

    def step(k, so_far):
        return combine(so_far, jax.tree.map(lambda part: part[k], everything))

    return lax.fori_loop(1, lax.axis_size(axis), step, first)


def with_halo(x, sides, width):
    for axis, dim in sides:
        peers, length = (lax.axis_size(axis), x.shape[dim])
        up = [(i, (i + 1) % peers) for i in range(peers - 1)]
        down = [(j, i) for i, j in up]
        last = lax.slice_in_dim(x, length - width, length, axis=dim)
        first = lax.slice_in_dim(x, 0, width, axis=dim)
        before = lax.ppermute(last, axis, up)
        after = lax.ppermute(first, axis, down)
        x = jnp.concatenate([before, x, after], axis=dim)
    return x


def silu_slope(pre_act):
    sigmoid_v = jax.nn.sigmoid(pre_act)
    return sigmoid_v * (1.0 + pre_act * (1.0 - sigmoid_v))


def split_heads(values, head_count):
    return values.reshape(values.shape[:-1] + (head_count, values.shape[-1] // head_count))


def combine_parts(part_a, part_b):
    top_a, sum_a, acc_a = part_a
    top_b, sum_b, acc_b = part_b
    top_score = jnp.maximum(top_a, top_b)
    fac_a = jnp.exp(top_a - top_score)
    fac_b = jnp.exp(top_b - top_score)
    head_count = top_score.shape[-1]
    merged = (
        split_heads(acc_a, head_count) * fac_a[..., None]
        + split_heads(acc_b, head_count) * fac_b[..., None]
    )
    return (top_score, sum_a * fac_a + sum_b * fac_b, merged.reshape(acc_a.shape))


def normalize(accum_out, totals):
    head_count = totals.shape[-1]
    return (
        (split_heads(accum_out, head_count) / totals[..., None])
        .reshape(accum_out.shape)
        .astype(jnp.bfloat16)
    )


def conv_apply(source, weight, bias_row, dilation, out_count):
    stacked = jnp.stack(
        [source[j * dilation : j * dilation + out_count] for j in range(KSIZE)], axis=2
    )
    return (
        jnp.einsum("tlji,jio->tlo", stacked, weight, preferred_element_type=jnp.float32) + bias_row
    )


def local(
    signal,
    pos_idx,
    live_count,
    latents,
    pos_table,
    w_in,
    w_kv,
    w_query,
    w_out,
    conv_weight,
    conv_bias,
    cotangent,
):
    con_dev = signal.shape[0]
    pat_dev = signal.shape[1] // PATCH
    model_width = w_query.shape[0]
    head_count = model_width // HD
    lat_rows = latents.shape[0]
    groups = lax.axis_size("contacts")
    lat_dev = lat_rows // groups
    owner_idx = lax.axis_index("contacts")
    is_valid = jnp.arange(con_dev, dtype=jnp.int32) < live_count[0]
    embedded = jnp.einsum(
        "cpt,td->pcd",
        signal.reshape(con_dev, pat_dev, PATCH),
        w_in,
        preferred_element_type=jnp.float32,
    )
    pos_rows = jnp.take(pos_table, pos_idx, axis=0).astype(jnp.float32)
    tokens = (embedded + pos_rows[None]).astype(jnp.bfloat16)
    keyval = jnp.dot(
        tokens.reshape(pat_dev * con_dev, model_width), w_kv, preferred_element_type=jnp.float32
    ).astype(jnp.bfloat16)
    keyval = keyval.reshape(pat_dev // 2, 2, con_dev, 2, head_count, HD)
    queries = (
        jnp.dot(latents, w_query, preferred_element_type=jnp.float32)
        .astype(jnp.bfloat16)
        .reshape(lat_rows, head_count, HD)
    )

    def masked_scores(key_block):
        scores = (
            jnp.einsum("ihe,pche->phic", queries, key_block, preferred_element_type=jnp.float32)
            * scale_dot
        )
        return jnp.where(is_valid, scores, neg_big)

    def attend(kv_block):
        scores = masked_scores(kv_block[:, :, 0])
        top_score = jnp.max(scores, axis=3)
        weights = jnp.where(is_valid, jnp.exp(scores - top_score[..., None]), 0.0)
        totals = jnp.sum(weights, axis=3)
        accum_out = jnp.einsum(
            "phic,pche->pihe",
            weights.astype(jnp.bfloat16),
            kv_block[:, :, 1],
            preferred_element_type=jnp.float32,
        )
        return (
            jnp.swapaxes(top_score, 1, 2),
            jnp.swapaxes(totals, 1, 2),
            accum_out.reshape(2, lat_rows, model_width),
        )

    top_score, totals, accum_out = lax.map(attend, keyval)
    top_score = top_score.reshape(pat_dev, lat_rows, head_count)
    totals = totals.reshape(pat_dev, lat_rows, head_count)
    accum_out = accum_out.reshape(pat_dev, lat_rows, model_width)
    top_all, total_all, acc_all = joined((top_score, totals, accum_out), "contacts", combine_parts)
    attended_all = normalize(acc_all, total_all)
    attended = lax.dynamic_slice_in_dim(attended_all, owner_idx * lat_dev, lat_dev, 1)
    start_x = (
        jnp.dot(
            attended.reshape(pat_dev * lat_dev, model_width),
            w_out,
            preferred_element_type=jnp.float32,
        )
        .astype(jnp.bfloat16)
        .reshape(pat_dev, lat_dev, model_width)
    )
    hidden_list = []
    current = start_x
    for layer_no in range(LAYERS):
        dilation = 2**layer_no
        padded = with_halo(current, (("tm", 0),), dilation * (KSIZE // 2))
        pre_act = conv_apply(padded, conv_weight[layer_no], conv_bias[layer_no], dilation, pat_dev)
        current = (current.astype(jnp.float32) + jax.nn.silu(pre_act)).astype(jnp.bfloat16)
        hidden_list.append(pre_act)
    grad_now = cotangent.astype(jnp.float32)
    for layer_no in reversed(range(LAYERS)):
        dilation = 2**layer_no
        grad_pre = (grad_now * silu_slope(hidden_list[layer_no])).astype(jnp.bfloat16)
        padded = with_halo(grad_pre, (("tm", 0),), dilation * (KSIZE // 2))
        stacked = jnp.stack(
            [
                padded[(KSIZE - 1 - j) * dilation : (KSIZE - 1 - j) * dilation + pat_dev]
                for j in range(KSIZE)
            ],
            axis=2,
        )
        grad_now = grad_now + jnp.einsum(
            "tljo,jio->tli", stacked, conv_weight[layer_no], preferred_element_type=jnp.float32
        )
    grad_att = lax.dot_general(
        grad_now.astype(jnp.bfloat16).reshape(pat_dev * lat_dev, model_width),
        w_out,
        (((1,), (1,)), ((), ())),
        preferred_element_type=jnp.float32,
    )
    grad_att = grad_att.astype(jnp.bfloat16).reshape(pat_dev, lat_dev, model_width)
    grad_all = lax.all_gather(grad_att, "contacts", axis=1, tiled=True)
    delta_row = jnp.sum(
        split_heads(grad_all.astype(jnp.float32), head_count)
        * split_heads(attended_all.astype(jnp.float32), head_count),
        axis=3,
    )

    def back_block(dq_sum, parts):
        kv_block, grad_block, top_block, total_block, delta_block = parts
        key_block = kv_block[:, :, 0]
        scores = masked_scores(key_block)
        top_now = jnp.swapaxes(top_block, 1, 2)
        total_now = jnp.swapaxes(total_block, 1, 2)
        prob_vals = jnp.where(
            is_valid, jnp.exp(scores - top_now[..., None]) / total_now[..., None], 0.0
        )
        grad_prob = jnp.einsum(
            "pihe,pche->phic",
            split_heads(grad_block, head_count),
            kv_block[:, :, 1],
            preferred_element_type=jnp.float32,
        )
        delta_now = jnp.swapaxes(delta_block, 1, 2)
        dscore = (prob_vals * (grad_prob - delta_now[..., None])).astype(jnp.bfloat16)
        return (
            dq_sum
            + jnp.einsum("phic,pche->ihe", dscore, key_block, preferred_element_type=jnp.float32),
            None,
        )

    pairs = pat_dev // 2
    dq_sum, unused = lax.scan(
        back_block,
        jnp.zeros((lat_rows, head_count, HD), jnp.float32),
        (
            keyval,
            grad_all.reshape(pairs, 2, lat_rows, model_width),
            top_all.reshape(pairs, 2, lat_rows, head_count),
            total_all.reshape(pairs, 2, lat_rows, head_count),
            delta_row.reshape(pairs, 2, lat_rows, head_count),
        ),
    )
    query_grad = lax.psum((dq_sum * scale_dot).reshape(lat_rows, model_width), ("contacts", "tm"))
    d_latents = lax.dot_general(
        query_grad.astype(jnp.bfloat16),
        w_query,
        (((1,), (1,)), ((), ())),
        preferred_element_type=jnp.float32,
    )
    return (current, d_latents)


def solution(mesh):
    in_specs = (
        P("contacts", "tm"),
        P("contacts"),
        P("contacts"),
        P(),
        P(),
        P(),
        P(),
        P(),
        P(),
        P(),
        P(),
        P("tm", "contacts", None),
    )
    out_specs = (P("tm", "contacts", None), P())
    return jax.shard_map(local, mesh=mesh, in_specs=in_specs, out_specs=out_specs, check_vma=False)
```

profile of v0, /device:TPU:1, one launch (start us, length us, event | category | flops | bytes accessed | tf_op | source)
XLA Modules:
  0.0 1136.9 jit_solution(8328710909862078384)
XLA Ops:
  9.6 3.9 gather_fusion
  15.5 4.0 reshape.142
  19.5 5.5 copy.76
  25.4 12.2 %while.46 = (s32[]{:T(128)}, f32[2,2,256,8]{2,3,1,0:T(8,128)S(1)}, f32[2,2,256,8]{2,3,1,0:T(8,128)S(1)}, f32[2,2,256,512]{3,2,1,0:T(8,128)}, bf16[2,2,256,2,8,64...) while((s32[]{:T(128)}, f32[2,2,256,8]{2,3,1,0:T(8,128)S(1)}, ...), condition=%wide.region_3.4_spmd.clone, body=%wide.region_0.3_spmd.clone.sunk | while | flops 277864704 | bytes 21349984 | solution.py:143
  39.8 73.7 %all-gather.7.cloned.1.call-done = f32[32,4,256,8]{2,3,1,0:T(8,128)} async-done(((f32[1,4,256,8]{2,3,1,0:T(8,128)}), f32[32,4,256,8]{2,3,1,0:T(8,128)}) %all-gather.7.cloned.1.call-update) | async-done | bytes 1048592 | tf_op jit(solution)/shard_map/all_gather | solution.py:15
  114.2 76.3 %all-gather.5.cloned.1.call-done = f32[32,4,256,8]{2,3,1,0:T(8,128)} async-done(((f32[1,4,256,8]{2,3,1,0:T(8,128)}), f32[32,4,256,8]{2,3,1,0:T(8,128)}) %all-gather.5.cloned.1.call-update) | async-done | bytes 1048592 | tf_op jit(solution)/shard_map/all_gather | solution.py:15
  191.3 434.8 %all-gather.9.cloned.1.call-done = f32[32,4,256,512]{3,2,1,0:T(8,128)} async-done(((f32[1,4,256,512]{3,2,1,0:T(8,128)}), f32[32,4,256,512]{3,2,1,0:T(8,128)}) %all-gather.9.cloned.1.call-update) | async-done | bytes 67108880 | tf_op jit(solution)/shard_map/all_gather | solution.py:15
  629.7 282.2 %while.45 = (s32[]{:T(128)}, f32[4,256,8]{1,2,0:T(8,128)S(1)}, f32[4,256,8]{1,2,0:T(8,128)S(1)}, f32[4,256,512]{1,2,0:T(8,128)}, f32[32,4,256,8]{2,3,1,0:T(8,128...) while((s32[]{:T(128)}, f32[4,256,8]{1,2,0:T(8,128)S(1)}, ...), condition=%wide.region_5.6_spmd, body=%wide.region_4.5_spmd.sunk | while | flops 1622021 | bytes 15007895 | solution.py:21
  635.5 3.2 fusion.147
  639.6 3.1 constant_dynamic-slice_fusion.10
  644.6 3.2 fusion.147
  653.7 3.2 fusion.147
  662.8 3.2 fusion.147
  671.9 3.2 fusion.147
  681.1 3.2 fusion.147
  690.2 3.2 fusion.147
  699.3 3.2 fusion.147
  708.4 3.2 fusion.147
  717.5 3.2 fusion.147
  726.6 3.2 fusion.147
  735.7 3.2 fusion.147
  744.8 3.2 fusion.147
  753.9 3.2 fusion.147
  763.0 3.2 fusion.147
  772.1 3.2 fusion.147
  781.2 3.2 fusion.147
  790.3 3.2 fusion.147
  799.4 3.2 fusion.147
  808.5 3.2 fusion.147
  817.6 3.2 fusion.147
  826.7 3.2 fusion.147
  835.8 3.2 fusion.147
  844.9 3.2 fusion.147
  854.0 3.2 fusion.147
  863.1 3.2 fusion.147
  872.2 3.2 fusion.147
  881.4 3.2 fusion.147
  890.5 3.2 fusion.147
  899.6 3.2 fusion.147
  908.7 3.2 fusion.147
  914.3 4.5 collective-permute-start
  935.6 3.6 collective-permute-start.5
  942.6 4.4 collective-permute-start.7
  950.5 69.0 %all-gather.11.cloned.1.call-done = bf16[4,256,512]{2,0,1:T(4,128)(2,1)} async-done(((bf16[4,8,512]{2,0,1:T(4,128)(2,1)}), bf16[4,256,512]{2,0,1:T(4,128)(2,1)}) %all-gather.11.cloned.1.call-update) | async-done | bytes 1048592 | tf_op jit(solution)/shard_map/all_gather | solution.py:189
  1022.1 23.4 %while.47 = (s32[]{:T(128)}, f32[256,8,64]{0,2,1:T(8,128)}, bf16[2,2,256,2,8,64]{2,5,1,4,3,0:T(8,128)(2,1)}, bf16[256,8,64]{0,2,1:T(8,128)(2,1)S(1)}, f32[2,2,25...) while((s32[]{:T(128)}, f32[256,8,64]{0,2,1:T(8,128)}, ...), condition=%wide.region_8.9_spmd.clone, body=%wide.region_7.8_spmd.clone.sunk | while | flops 411304192 | bytes 15189387 | solution.py:220
  1028.5 5.3 fusion.155
  1040.1 5.5 fusion.155
  1046.7 82.5 %all-reduce.1 = bf16[256,512]{0,1:T(8,128)(2,1)S(1)} all-reduce(f32[256,512]{0,1:T(8,128)S(1)} %bitcast.319), channel_id=1, replica_groups=mesh['contacts'=32,'tm'=8] {'contacts','tm'}, use_global_device_ids=true, to_apply=%region_9.10 | all-reduce | flops 131072 | bytes 786432 | tf_op jit(solution)/shard_map/psum | solution.py:231
  (208 shorter events, 245.8 us)
Async XLA Ops:
  7.2 7.0 copy-start
  7.2 6.5 copy-start.6
  7.2 106.3 %all-gather.7.cloned.1.call-start = ((), (), s32[]{:S(2)}) async-start(), calls=%async_computation.1 | async-start | bytes 1081344 | tf_op jit(solution)/shard_map/all_gather | solution.py:15
  19.4 5.5 copy-start.1
  19.4 5.5 copy-start.5
  37.6 0.6 copy-start.8
  37.6 0.7 copy-start.7
  38.2 152.3 %all-gather.5.cloned.1.call-start = ((), (), s32[]{:S(2)}) async-start(), calls=%async_computation | async-start | bytes 1081344 | tf_op jit(solution)/shard_map/all_gather | solution.py:15
  39.0 587.1 %all-gather.9.cloned.1.call-start = ((), (), s32[]{:S(2)}) async-start(), calls=%async_computation.2 | async-start | bytes 69206016 | tf_op jit(solution)/shard_map/all_gather | solution.py:15
  39.7 979.8 %all-gather.11.cloned.1.call-start = ((), (), s32[]{:S(2)}) async-start(), calls=%async_computation.3 | async-start | bytes 1081344 | tf_op jit(solution)/shard_map/all_gather | solution.py:189
  911.9 2.2 copy-start.3
  911.9 8.9 copy-start.9
  914.1 18.5 %copy-start.4 = (bf16[2,3,512,512]{3,2,1,0:T(8,128)(2,1)S(1)}, bf16[2,3,512,512]{3,2,1,0:T(8,128)(2,1)}, u32[]{:S(2)}) copy-start(bf16[2,3,512,512]{3,2,1,0:T(8,128)(2,1)} %param.27) | copy-start | bytes 9437188
  914.1 18.6 %copy-start.10 = (bf16[4,8,512]{2,1,0:T(8,128)(2,1)S(1)}, bf16[4,8,512]{2,1,0:T(8,128)(2,1)}, u32[]{:S(2)}) copy-start(bf16[4,8,512]{2,1,0:T(8,128)(2,1)} %param.29) | copy-start | bytes 98308
  914.3 6.5 collective-permute-start
  918.9 5.0 collective-permute-start.1
  925.7 4.3 collective-permute-start.2
  927.6 5.1 collective-permute-start.3
  933.7 5.6 collective-permute-start.4
  935.6 4.5 collective-permute-start.5
  940.7 6.3 collective-permute-start.6
  942.6 5.0 collective-permute-start.7
  1045.6 83.6 %copy-start.2 = (bf16[512,512]{1,0:T(8,128)(2,1)S(1)}, bf16[512,512]{1,0:T(8,128)(2,1)}, u32[]{:S(2)}) copy-start(bf16[512,512]{1,0:T(8,128)(2,1)} %param.25) | copy-start | bytes 1572868
Sparse Core Ops, SparseCore 0:
  38.4 75.0 all-gather.6
  116.6 73.8 all-gather.4
  193.1 432.8 all-gather.8
  950.6 68.8 all-gather.10
where the time goes:
time: 1140 us
  waiting for transfers between devices  662 us (58%)
  local copies, waits for them, and re-layouts  191 us (17%)
  other arithmetic  136 us (12%)
  blocking collectives  82.5 us (7%)
  matrix products  28.2 us (2%)
  starting transfers between devices  22.8 us (2%)
  between operations  14.1 us (1%)
    all_gather x3, waiting for transfers between devices, joined(): everything = jax.tree.map(lambda part: lax.all_gather(part, axis), x)  585 us
    dynamic_slice x62, local copies, waits for them, and re-layouts, step(): return combine(so_far, jax.tree.map(lambda part: part[k], everything))  156 us
    add x31, other arithmetic, combine_parts(): split_heads(acc_a, head_count) * fac_a[..., None]  100 us
    psum x1, blocking collectives, local(): lax.psum((dq_sum * scale_dot).reshape(lat_rows, model_width), ('contacts'...  82.5 us
    all_gather x1, waiting for transfers between devices, local(): grad_all = lax.all_gather(grad_att, 'contacts', axis=1, tiled=True)  69 us
    add x31, other arithmetic, combine_parts(): sum_a * fac_a + sum_b * fac_b  25.1 us
  transfers between devices with their start and end apart: 12, of which 8 were waited for; matrix products, arithmetic and copies ran while one was open for 0% of the time, Pallas kernels for 0%

commit v1 on v0

--- a/solution.py
+++ b/solution.py
@@ -186,7 +186,9 @@
         preferred_element_type=jnp.float32,
     )
     grad_att = grad_att.astype(jnp.bfloat16).reshape(pat_dev, lat_dev, model_width)
-    grad_all = lax.all_gather(grad_att, "contacts", axis=1, tiled=True)
+    grad_all = jnp.concatenate(
+        lax.all_to_all(jnp.stack([grad_att] * lax.axis_size("contacts")), "contacts", 0, 0), axis=1
+    )
     delta_row = jnp.sum(
         split_heads(grad_all.astype(jnp.float32), head_count)
         * split_heads(attended_all.astype(jnp.float32), head_count),

time: 1140 us -> 1110 us (0.974)
  waiting for transfers between devices: 662 us -> 619 us
    all_gather x1 -> x0, waiting for transfers between devices: 69 us -> none  [local(): grad_all = lax.all_gather(grad_att, 'contacts', axis=1, tiled=True)]
    all_to_all x0 -> x1, waiting for transfers between devices: none -> 25.2 us  [local(): lax.all_to_all(jnp.stack([grad_att] * lax.axis_size('contacts')), 'contac...]
where the time goes in v1:
time: 1110 us; the launch traced here: 1100 us
  waiting for transfers between devices  619 us (56%)
  local copies, waits for them, and re-layouts  194 us (17%)
  other arithmetic  142 us (13%)
  blocking collectives  77.1 us (7%)
  starting transfers between devices  28.2 us (3%)
  matrix products  27.9 us (3%)
  between operations  14.1 us (1%)
    all_gather x3, waiting for transfers between devices, joined(): everything = jax.tree.map(lambda part: lax.all_gather(part, axis), x)  585 us
    dynamic_slice x62, local copies, waits for them, and re-layouts, step(): return combine(so_far, jax.tree.map(lambda part: part[k], everything))  156 us
    add x31, other arithmetic, combine_parts(): split_heads(acc_a, head_count) * fac_a[..., None]  100 us
    psum x1, blocking collectives, local(): lax.psum((dq_sum * scale_dot).reshape(lat_rows, model_width), ('contacts'...  77.1 us
    all_to_all x1, waiting for transfers between devices, local(): lax.all_to_all(jnp.stack([grad_att] * lax.axis_size('contacts')), 'contac...  25.2 us
    add x31, other arithmetic, combine_parts(): sum_a * fac_a + sum_b * fac_b  25.1 us
  transfers between devices with their start and end apart: 12, of which 8 were waited for; matrix products, arithmetic and copies ran while one was open for 0% of the time, Pallas kernels for 0%

profile of v1, /device:TPU:1, one launch (start us, length us, event | category | flops | bytes accessed | tf_op | source)
XLA Modules:
  0.0 1102.4 jit_solution(16979741276371553746)
XLA Ops:
  9.6 3.9 gather_fusion
  15.5 4.0 reshape.153
  19.5 5.5 copy.78
  25.4 12.2 %while.46 = (s32[]{:T(128)}, f32[2,2,256,8]{2,3,1,0:T(8,128)S(1)}, f32[2,2,256,8]{2,3,1,0:T(8,128)S(1)}, f32[2,2,256,512]{3,2,1,0:T(8,128)}, bf16[2,2,256,2,8,64...) while((s32[]{:T(128)}, f32[2,2,256,8]{2,3,1,0:T(8,128)S(1)}, ...), condition=%wide.region_3.4_spmd.clone, body=%wide.region_0.3_spmd.clone.sunk | while | flops 277864704 | bytes 21349984 | solution.py:143
  39.8 73.7 %all-gather.6.cloned.1.call-done = f32[32,4,256,8]{2,3,1,0:T(8,128)} async-done(((f32[1,4,256,8]{2,3,1,0:T(8,128)}), f32[32,4,256,8]{2,3,1,0:T(8,128)}) %all-gather.6.cloned.1.call-update) | async-done | bytes 1048592 | tf_op jit(solution)/shard_map/all_gather | solution.py:15
  114.3 76.3 %all-gather.4.cloned.1.call-done = f32[32,4,256,8]{2,3,1,0:T(8,128)} async-done(((f32[1,4,256,8]{2,3,1,0:T(8,128)}), f32[32,4,256,8]{2,3,1,0:T(8,128)}) %all-gather.4.cloned.1.call-update) | async-done | bytes 1048592 | tf_op jit(solution)/shard_map/all_gather | solution.py:15
  191.3 434.8 %all-gather.8.cloned.1.call-done = f32[32,4,256,512]{3,2,1,0:T(8,128)} async-done(((f32[1,4,256,512]{3,2,1,0:T(8,128)}), f32[32,4,256,512]{3,2,1,0:T(8,128)}) %all-gather.8.cloned.1.call-update) | async-done | bytes 67108880 | tf_op jit(solution)/shard_map/all_gather | solution.py:15
  629.7 281.9 %while.45 = (s32[]{:T(128)}, f32[4,256,8]{1,2,0:T(8,128)S(1)}, f32[4,256,8]{1,2,0:T(8,128)S(1)}, f32[4,256,512]{1,2,0:T(8,128)}, f32[32,4,256,8]{2,3,1,0:T(8,128...) while((s32[]{:T(128)}, f32[4,256,8]{1,2,0:T(8,128)S(1)}, ...), condition=%wide.region_5.6_spmd, body=%wide.region_4.5_spmd.sunk | while | flops 1622021 | bytes 15007895 | solution.py:21
  635.5 3.2 fusion.147
  644.6 3.2 fusion.147
  653.7 3.2 fusion.147
  662.8 3.2 fusion.147
  671.9 3.2 fusion.147
  681.0 3.2 fusion.147
  690.1 3.2 fusion.147
  699.2 3.2 fusion.147
  708.3 3.2 fusion.147
  717.4 3.2 fusion.147
  726.5 3.2 fusion.147
  735.6 3.2 fusion.147
  744.7 3.2 fusion.147
  753.8 3.2 fusion.147
  762.9 3.2 fusion.147
  772.0 3.2 fusion.147
  781.0 3.2 fusion.147
  790.1 3.2 fusion.147
  799.2 3.2 fusion.147
  808.3 3.2 fusion.147
  817.4 3.2 fusion.147
  826.5 3.2 fusion.147
  835.6 3.2 fusion.147
  853.8 3.2 fusion.147
  862.9 3.2 fusion.147
  872.0 3.2 fusion.147
  881.1 3.2 fusion.147
  890.2 3.2 fusion.147
  899.3 3.2 fusion.147
  908.4 3.2 fusion.147
  914.0 4.5 collective-permute-start
  935.3 3.6 collective-permute-start.5
  942.4 4.2 collective-permute-start.7
  950.6 5.7 all-to-all-start
  958.8 25.2 %all-to-all-done = bf16[32,4,8,512]{3,2,1,0:T(8,128)(2,1)} async-done(((bf16[32,4,8,512]{3,2,1,0:T(8,128)(2,1)}), bf16[32,4,8,512]{3,2,1,0:T(8,128)(2,1)}, u32[]{:S(2)}, u32[]{:S(2)}) %all-to-all-start) | async-done | bytes 1048608 | tf_op jit(solution)/shard_map/all_to_all | solution.py:190
  988.9 4.6 multiply_reduce_fusion
  993.8 22.6 %while.47 = (s32[]{:T(128)}, f32[256,8,64]{0,2,1:T(8,128)}, bf16[2,2,256,2,8,64]{2,5,1,4,3,0:T(8,128)(2,1)}, bf16[256,8,64]{0,2,1:T(8,128)(2,1)S(1)}, f32[2,2,25...) while((s32[]{:T(128)}, f32[256,8,64]{0,2,1:T(8,128)}, ...), condition=%wide.region_8.9_spmd.clone, body=%wide.region_7.8_spmd.clone.sunk | while | flops 411304192 | bytes 16205195 | solution.py:222
  999.9 5.2 fusion.155
  1011.1 5.3 fusion.155
  1017.6 77.1 %all-reduce.1 = bf16[256,512]{0,1:T(8,128)(2,1)S(1)} all-reduce(f32[256,512]{0,1:T(8,128)S(1)} %bitcast.324), channel_id=1, replica_groups=mesh['contacts'=32,'tm'=8] {'contacts','tm'}, use_global_device_ids=true, to_apply=%region_9.10 | all-reduce | flops 131072 | bytes 786432 | tf_op jit(solution)/shard_map/psum | solution.py:233
  (212 shorter events, 257.2 us)
Async XLA Ops:
  7.2 7.0 copy-start
  7.2 6.5 copy-start.7
  7.2 106.3 %all-gather.6.cloned.1.call-start = ((), (), s32[]{:S(2)}) async-start(), calls=%async_computation.2 | async-start | bytes 1081344 | tf_op jit(solution)/shard_map/all_gather | solution.py:15
  19.5 5.5 copy-start.2
  19.5 5.5 copy-start.6
  37.6 0.6 copy-start.9
  37.6 0.7 copy-start.8
  38.3 152.3 %all-gather.4.cloned.1.call-start = ((), (), s32[]{:S(2)}) async-start(), calls=%async_computation.1 | async-start | bytes 1081344 | tf_op jit(solution)/shard_map/all_gather | solution.py:15
  39.0 587.0 %all-gather.8.cloned.1.call-start = ((), (), s32[]{:S(2)}) async-start(), calls=%async_computation.3 | async-start | bytes 69206016 | tf_op jit(solution)/shard_map/all_gather | solution.py:15
  911.6 2.2 copy-start.4
  911.6 8.9 copy-start.10
  913.4 18.9 %copy-start.11 = (bf16[4,8,512]{2,1,0:T(8,128)(2,1)S(1)}, bf16[4,8,512]{2,1,0:T(8,128)(2,1)}, u32[]{:S(2)}) copy-start(bf16[4,8,512]{2,1,0:T(8,128)(2,1)} %param.29) | copy-start | bytes 98308
  913.8 18.5 %copy-start.5 = (bf16[2,3,512,512]{3,2,1,0:T(8,128)(2,1)S(1)}, bf16[2,3,512,512]{3,2,1,0:T(8,128)(2,1)}, u32[]{:S(2)}) copy-start(bf16[2,3,512,512]{3,2,1,0:T(8,128)(2,1)} %param.27) | copy-start | bytes 9437188
  914.0 6.5 collective-permute-start
  918.6 5.0 collective-permute-start.1
  925.4 4.3 collective-permute-start.2
  927.3 5.1 collective-permute-start.3
  933.4 5.6 collective-permute-start.4
  935.3 4.5 collective-permute-start.5
  940.4 6.1 collective-permute-start.6
  942.4 5.0 collective-permute-start.7
  950.6 33.3 %all-to-all-start = ((bf16[32,4,8,512]{3,2,1,0:T(8,128)(2,1)}), bf16[32,4,8,512]{3,2,1,0:T(8,128)(2,1)}, u32[]{:S(2)}, u32[]{:S(2)}) async-start(bf16[32,4,8,512]{3,2,1,0:T(8,128)(2,1)} %stack.63), calls=%async_computation | async-start | bytes 2097152 | tf_op jit(solution)/shard_map/all_to_all | solution.py:190
  993.8 100.9 %copy-start.3 = (bf16[512,512]{1,0:T(8,128)(2,1)S(1)}, bf16[512,512]{1,0:T(8,128)(2,1)}, u32[]{:S(2)}) copy-start(bf16[512,512]{1,0:T(8,128)(2,1)} %param.25) | copy-start | bytes 1572868
  1016.4 79.5 %copy-start.1 = (bf16[512,1024]{1,0:T(8,128)(2,1)S(1)}, bf16[512,1024]{1,0:T(8,128)(2,1)}, u32[]{:S(2)}) copy-start(bf16[512,1024]{1,0:T(8,128)(2,1)} %param.24) | copy-start | bytes 3145732
Sparse Core Ops, SparseCore 0:
  38.4 75.0 all-gather.5
  116.7 73.8 all-gather.3
  193.1 432.8 all-gather.7
